TPU v7x, 256 devices: a whole 4x4x8 slice. The times are simulated.
256 devices in a mesh: expert: 8 (over y, core), tensor: 32 (over z, x).
Axes of the slice: x: 4, y: 4, z: 8, core: 2. Of those that a mesh axis runs over, the one named last changes fastest.
Arguments:
- tokens: bfloat16 [2048, 6144], P('expert', 'tensor'), may hold values from -6 to 6
- expert_ids: int32 [2048, 2], P('expert'), may hold values from 0 to 7, all different within a row; in each aligned block of 256 rows (0 to 255, 256 to 511, ...) at most 96 rows name the same one
- gate_prob: float32 [2048, 2], P('expert'), may hold values from 0.1 to 1
- w_gate: bfloat16 [8, 6144, 8192], P('expert', None, 'tensor'), may hold values from -0.078125 to 0.078125
- w_up: bfloat16 [8, 6144, 8192], P('expert', None, 'tensor'), may hold values from -0.078125 to 0.078125
- w_down: bfloat16 [8, 8192, 6144], P('expert', 'tensor'), may hold values from -0.125 to 0.125
Outputs:
- mixed: bfloat16 [2048, 6144], P('expert', 'tensor')
Inputs may be any that keep to these rules, and one draw needn't show every extreme that they name: `expert_ids`: the two experts of a row differ. Within the rows of one index of expert (aligned blocks of 256 rows) no expert is named by more than 96 rows, and in every draw some expert is named by exactly 96 rows of some block.
All inputs are finite; a program needn't handle non-finite values.
Results may differ from a plain program's by a relative error of at most 0.017.
Values may be sent and summed in bfloat16 or wider, within the bound.
No kernel may reach another device: no remote copies, remote signals or barrier semaphores. Data moves between devices by JAX's collectives and lax.ppermute only.
A program may use at most 64 MiB of HBM per device.

v0:
```python
import jax
import jax.numpy as jnp
from jax import lax
from jax.sharding import PartitionSpec as P


def slot_table(ids, experts, cap):
    flat = ids.reshape(-1)
    onehot = (flat[:, None] == jnp.arange(experts, dtype=jnp.int32)[None, :]).astype(jnp.int32)
    before = jnp.cumsum(onehot, axis=0) - onehot
    position = jnp.sum(before * onehot, axis=1)
    slot = flat * cap + position
    match = slot[None, :] == jnp.arange(experts * cap, dtype=jnp.int32)[:, None]
    which = jnp.arange(flat.shape[0], dtype=jnp.int32) // 2
    owner = jnp.max(jnp.where(match, which[None, :], -1), axis=1)
    return (slot, owner)


def fill_slots(block, owner):
    picked = jnp.take(block, jnp.maximum(owner, 0), axis=0)
    return jnp.where((owner >= 0)[:, None], picked, jnp.zeros_like(picked))


def local(tokens, expert_ids, gate_prob, w_gate, w_up, w_down):
    experts = lax.axis_size("expert")
    group_rows = tokens.shape[0]
    cap = 3 * group_rows // experts
    slot, owner = slot_table(expert_ids, experts, cap)
    gate_mat = w_gate[0]
    up_mat = w_up[0]
    down_mat = w_down[0]
    columns = tokens.shape[1]
    sending = fill_slots(tokens, owner).reshape(experts, cap, columns)
    arrived = lax.all_to_all(sending, "expert", split_axis=0, concat_axis=0, tiled=True).reshape(
        experts * cap, columns
    )
    piece = lax.all_gather(arrived, "tensor", axis=1, tiled=True)
    gate = jnp.dot(piece, gate_mat, preferred_element_type=jnp.float32)
    up = jnp.dot(piece, up_mat, preferred_element_type=jnp.float32)
    hidden = (jax.nn.silu(gate) * up).astype(jnp.bfloat16)
    partial_out = jnp.dot(hidden, down_mat, preferred_element_type=jnp.float32)
    summed = lax.psum_scatter(
        partial_out.astype(jnp.bfloat16), "tensor", scatter_dimension=1, tiled=True
    ).astype(jnp.float32)
    columns = summed.shape[1]
    returned = lax.all_to_all(
        summed.reshape(experts, cap, columns).astype(jnp.bfloat16),
        "expert",
        split_axis=0,
        concat_axis=0,
        tiled=True,
    ).astype(jnp.float32)
    table = returned.reshape(experts * cap, columns)
    picked = jnp.take(table, slot, axis=0).reshape(group_rows, 2, columns)
    mixed = jnp.sum(gate_prob[:, :, None] * picked, axis=1)
    return mixed.astype(jnp.bfloat16)


def solution(mesh):
    return jax.shard_map(
        local,
        mesh=mesh,
        in_specs=(
            P("expert", "tensor"),
            P("expert", None),
            P("expert", None),
            P("expert", None, "tensor"),
            P("expert", None, "tensor"),
            P("expert", "tensor", None),
        ),
        out_specs=P("expert", "tensor"),
        check_vma=False,
    )
```

profile of v0, /device:TPU:1, one launch (start us, length us, event | category | flops | bytes accessed | tf_op | source)
XLA Modules:
  0.0 413.5 jit_solution(16867759176059031204)
XLA Ops:
  6.5 0.0 copy-start
  6.5 0.0 all-gather.2.cloned.1.call-start
  6.5 1.0 copy.36
  7.5 0.1 eq.39
  7.7 0.1 reshape.131
  7.8 1.1 reduce-window.6
  9.0 0.2 slice_reduce_fusion
  9.2 0.1 fusion.12
  9.3 0.3 select_reduce_fusion
  9.6 0.1 ge.29
  9.7 0.1 le.31
  9.8 1.0 copy.40
  10.8 3.3 gather_fusion
  14.1 1.3 select_select_fusion
  15.4 13.8 %all_to_all.10 = bf16[8,96,192]{2,1,0:T(8,128)(2,1)S(1)} all-to-all(bf16[8,96,192]{2,1,0:T(8,128)(2,1)S(1)} %select_select_fusion), channel_id=1, replica_groups=mesh['expert'=8,'tensor'=32] {'expert'}, dimensions={0} | all-to-all | bytes 589824 | tf_op jit(solution)/shard_map/all_to_all | solution.py:34
  29.2 0.9 copy.46
  30.0 0.0 all-gather.2.cloned.1.call-update
  30.1 0.0 reduce-scatter.2.cloned.1.call-start
  30.1 103.6 %all-gather.2.cloned.1.call-done = bf16[768,6144]{0,1:T(8,128)(2,1)} async-done(((bf16[768,192]{0,1:T(8,128)(2,1)}), bf16[768,6144]{0,1:T(8,128)(2,1)}) %all-gather.2.cloned.1.call-update) | async-done | bytes 9437200 | tf_op jit(solution)/shard_map/all_gather | solution.py:37
  133.7 0.0 copy-start.1
  133.7 0.0 copy-start.6
  133.7 6.3 %fusion.3 = f32[768,256]{1,0:T(8,128)S(1)} fusion(bf16[768,6144]{0,1:T(8,128)(2,1)} %all-gather.2.cloned.1.call-done, bf16[1,6144,256]{2,1,0:T(8,128)(2,1)} %param.9), kind=kOutput, calls=%fused_computation.6 | convolution fusion | flops 2415919104 | bytes 13369344 | tf_op jit(solution)/shard_map/dot_general | solution.py:38
  140.1 1.0 copy-done.1
  141.1 0.9 copy-done.6
  142.0 2.7 fusion.8
  144.6 0.0 copy-done
  144.6 5.1 %convolution_convert_fusion = bf16[768,6144]{0,1:T(8,128)(2,1)} fusion(bf16[768,256]{1,0:T(8,128)(2,1)S(1)} %fusion.8, bf16[1,256,6144]{2,1,0:T(8,128)(2,1)S(1)} %copy-done), kind=kOutput, calls=%fused_computation.2 | convolution fusion | flops 2420637696 | bytes 12976128 | tf_op jit(solution)/shard_map/dot_general | solution.py:41
  149.7 0.0 copy-start.4
  149.7 0.0 copy-start.5
  149.7 0.0 reduce-scatter.2.cloned.1.call-update
  149.8 0.1 reduce_sum.23
  149.9 0.5 copy-done.4
  150.4 0.1 copy.44
  150.6 0.1 mul.53
  150.7 0.1 copy.38
  150.8 0.8 copy.39
  151.6 0.0 copy-done.5
  151.6 0.8 copy.35
  152.4 225.5 %reduce-scatter.2.cloned.1.call-done = bf16[768,192]{0,1:T(8,128)(2,1)} async-done(((bf16[768,6144]{0,1:T(8,128)(2,1)}), bf16[768,192]{0,1:T(8,128)(2,1)}) %reduce-scatter.2.cloned.1.call-update) | async-done | bytes 294928 | tf_op jit(solution)/shard_map/reduce_scatter | solution.py:42
  377.9 1.4 convert_element_type.26
  379.3 0.8 copy.42
  380.1 9.0 %all-to-all-start.1 = ((bf16[8,96,192]{1,2,0:T(8,128)(2,1)}), bf16[8,96,192]{1,2,0:T(8,128)(2,1)S(1)}, u32[]{:S(2)}, u32[]{:S(2)}) async-start(bf16[8,96,192]{1,2,0:T(8,128)(2,1)} %copy.42), calls=%async_computation.2 | async-start | bytes 786432 | tf_op jit(solution)/shard_map/all_to_all | solution.py:46
  389.2 7.7 %all-to-all-done.1 = bf16[8,96,192]{1,2,0:T(8,128)(2,1)S(1)} async-done(((bf16[8,96,192]{1,2,0:T(8,128)(2,1)}), bf16[8,96,192]{1,2,0:T(8,128)(2,1)S(1)}, u32[]{:S(2)}, u32[]{:S(2)}) %all-to-all-start.1) | async-done | bytes 294944 | tf_op jit(solution)/shard_map/all_to_all | solution.py:46
  396.8 1.1 copy.43
  397.9 0.0 copy-start.2
  397.9 0.0 copy-start.3
  397.9 3.4 gather_fusion.1
  401.3 2.1 gather.15
  403.5 0.0 copy-done.2
  403.5 0.0 copy-done.3
  403.5 2.4 multiply_reduce_fusion
  405.9 0.7 copy.45
  (11 shorter events, 0.1 us)
Async XLA Ops:
  6.5 138.1 %copy-start = (bf16[1,256,6144]{2,1,0:T(8,128)(2,1)S(1)}, bf16[1,256,6144]{2,1,0:T(8,128)(2,1)}, u32[]{:S(2)}) copy-start(bf16[1,256,6144]{2,1,0:T(8,128)(2,1)} %param.11) | copy-start | bytes 9437188
  6.5 127.2 %all-gather.2.cloned.1.call-start = ((), (), s32[]{:S(2)}) async-start(), calls=%async_computation.3 | async-start | bytes 9732096 | tf_op jit(solution)/shard_map/all_gather | solution.py:37
  30.1 347.9 %reduce-scatter.2.cloned.1.call-start = ((), (), s32[]{:S(2)}) async-start(), calls=%async_computation.4 | async-start | bytes 9732096 | tf_op jit(solution)/shard_map/reduce_scatter | solution.py:42
  133.7 7.3 %copy-start.1 = (bf16[768,6144]{0,1:T(8,128)(2,1)S(1)}, bf16[768,6144]{0,1:T(8,128)(2,1)}, u32[]{:S(2)}) copy-start(bf16[768,6144]{0,1:T(8,128)(2,1)} %all-gather.2.cloned.1.call-done) | copy-start | bytes 28311556
  133.7 8.2 %copy-start.6 = (bf16[1,6144,256]{2,1,0:T(8,128)(2,1)S(1)}, bf16[1,6144,256]{2,1,0:T(8,128)(2,1)}, u32[]{:S(2)}) copy-start(bf16[1,6144,256]{2,1,0:T(8,128)(2,1)} %param.10) | copy-start | bytes 9437188
  149.7 0.7 copy-start.4
  149.7 1.9 copy-start.5
  380.1 16.7 %all-to-all-start.1 = ((bf16[8,96,192]{1,2,0:T(8,128)(2,1)}), bf16[8,96,192]{1,2,0:T(8,128)(2,1)S(1)}, u32[]{:S(2)}, u32[]{:S(2)}) async-start(bf16[8,96,192]{1,2,0:T(8,128)(2,1)} %copy.42), calls=%async_computation.2 | async-start | bytes 786432 | tf_op jit(solution)/shard_map/all_to_all | solution.py:46
  397.9 5.6 %copy-start.2 = (f32[256,2]{1,0:T(8,128)S(1)}, f32[256,2]{1,0:T(8,128)}, u32[]{:S(2)}) copy-start(f32[256,2]{1,0:T(8,128)} %copy.35) | copy-start | bytes 6148
  397.9 5.6 %copy-start.3 = (pred[256,2]{1,0:T(8,128)(4,1)S(1)}, pred[256,2]{1,0:T(8,128)(4,1)}, u32[]{:S(2)}) copy-start(pred[256,2]{1,0:T(8,128)(4,1)} %copy.39) | copy-start | bytes 1540
Sparse Core Ops, SparseCore 0:
  30.2 103.4 all-gather.1
  149.9 228.0 reduce-scatter.1
where the time goes:
time: 414 us
  waiting for transfers between devices  337 us (81%)
  local copies, waits for them, and re-layouts  20.9 us (5%)
  matrix products  14.1 us (3%)
  blocking collectives  13.8 us (3%)
  between operations  13.6 us (3%)
  starting transfers between devices  9.05 us (2%)
  other arithmetic  5.31 us (1%)
    reduce_scatter x1, waiting for transfers between devices, local(): lax.psum_scatter(partial_out.astype(jnp.bfloat16), 'tensor', scatter_dime...  226 us
    all_gather x1, waiting for transfers between devices, local(): piece = lax.all_gather(arrived, 'tensor', axis=1, tiled=True)  104 us
    all_to_all x1, blocking collectives, local(): lax.all_to_all(sending, 'expert', split_axis=0, concat_axis=0, tiled=True)  13.8 us
    all_to_all x1, starting transfers between devices, local(): lax.all_to_all(summed.reshape(experts, cap, columns).astype(jnp.bfloat16)...  9 us
  transfers between devices with their start and end apart: 3, of which 3 were waited for; matrix products, arithmetic and copies ran while one was open for 1% of the time, Pallas kernels for 0%

commit v1 on v0

--- a/solution.py
+++ b/solution.py
@@ -34,7 +34,9 @@
     arrived = lax.all_to_all(sending, "expert", split_axis=0, concat_axis=0, tiled=True).reshape(
         experts * cap, columns
     )
-    piece = lax.all_gather(arrived, "tensor", axis=1, tiled=True)
+    piece = jnp.concatenate(
+        lax.all_to_all(jnp.stack([arrived] * lax.axis_size("tensor")), "tensor", 0, 0), axis=1
+    )
     gate = jnp.dot(piece, gate_mat, preferred_element_type=jnp.float32)
     up = jnp.dot(piece, up_mat, preferred_element_type=jnp.float32)
     hidden = (jax.nn.silu(gate) * up).astype(jnp.bfloat16)

time: 414 us -> 524 us (1.27)
  blocking collectives: 13.8 us -> 231 us
  waiting for transfers between devices: 337 us -> 233 us
    all_to_all x0 -> x1, blocking collectives: none -> 217 us  [local(): lax.all_to_all(jnp.stack([arrived] * lax.axis_size('tensor')), 'tensor',...]
    all_gather x1 -> x0, waiting for transfers between devices: 104 us -> none  [local(): piece = lax.all_gather(arrived, 'tensor', axis=1, tiled=True)]
  transfers between devices with their start and end apart: 3 -> 2, of which waited for: 3 -> 2; matrix products, arithmetic and copies ran while one was open for 1% -> 0% of each run, Pallas kernels for 0% -> 0%
where the time goes in v1:
time: 524 us; the launch traced here: 523 us
  waiting for transfers between devices  233 us (44%)
  blocking collectives  231 us (44%)
  local copies, waits for them, and re-layouts  21 us (4%)
  between operations  13.6 us (3%)
  matrix products  10.4 us (2%)
  starting transfers between devices  9 us (2%)
  other arithmetic  5.31 us (1%)
    reduce_scatter x1, waiting for transfers between devices, local(): lax.psum_scatter(partial_out.astype(jnp.bfloat16), 'tensor', scatter_dime...  225 us
    all_to_all x1, blocking collectives, local(): lax.all_to_all(jnp.stack([arrived] * lax.axis_size('tensor')), 'tensor',...  217 us
    all_to_all x1, blocking collectives, local(): lax.all_to_all(sending, 'expert', split_axis=0, concat_axis=0, tiled=True)  13.8 us
  transfers between devices with their start and end apart: 2, of which 2 were waited for; matrix products, arithmetic and copies ran while one was open for 0% of the time, Pallas kernels for 0%

profile of v1, /device:TPU:1, one launch (start us, length us, event | category | flops | bytes accessed | tf_op | source)
XLA Modules:
  0.0 523.1 jit_solution(12169938692920097005)
XLA Ops:
  6.5 0.0 copy-start
  6.5 0.0 reduce-scatter.2.cloned.1.call-start
  6.5 1.0 copy.37
  7.5 0.1 eq.39
  7.7 0.1 reshape.136
  7.8 1.1 reduce-window.6
  9.0 0.2 slice_reduce_fusion
  9.2 0.1 fusion.12
  9.3 0.3 select_reduce_fusion
  9.6 0.1 ge.29
  9.7 0.1 le.31
  9.8 1.0 copy.41
  10.8 3.3 gather_fusion
  14.1 1.3 select_select_fusion
  15.4 13.8 %all_to_all.15 = bf16[8,96,192]{2,1,0:T(8,128)(2,1)S(1)} all-to-all(bf16[8,96,192]{2,1,0:T(8,128)(2,1)S(1)} %select_select_fusion), channel_id=1, replica_groups=mesh['expert'=8,'tensor'=32] {'expert'}, dimensions={0} | all-to-all | bytes 589824 | tf_op jit(solution)/shard_map/all_to_all | solution.py:34
  29.2 0.9 copy.42
  30.0 2.0 stack.3
  32.1 0.0 copy-start.1
  32.1 217.0 %all_to_all.16 = bf16[32,768,192]{1,2,0:T(8,128)(2,1)S(1)} all-to-all(bf16[32,768,192]{1,2,0:T(8,128)(2,1)S(1)} %stack.3), channel_id=1, replica_groups=mesh['expert'=8,'tensor'=32] {'tensor'}, dimensions={0} | all-to-all | bytes 18874368 | tf_op jit(solution)/shard_map/all_to_all | solution.py:38
  249.1 0.0 copy-done.1
  249.1 0.0 copy-start.6
  249.1 2.6 fusion.3
  251.7 0.0 copy-done.6
  251.7 2.7 fusion.8
  254.4 0.0 copy-done
  254.4 5.1 convolution_convert_fusion
  259.5 0.0 copy-start.4
  259.5 0.0 copy-start.5
  259.5 0.0 reduce-scatter.2.cloned.1.call-update
  259.5 0.1 reduce_sum.23
  259.7 0.5 copy-done.4
  260.2 0.1 copy.45
  260.3 0.1 mul.53
  260.5 0.1 copy.39
  260.6 0.8 copy.40
  261.3 0.0 copy-done.5
  261.3 0.8 copy.36
  262.1 225.4 %reduce-scatter.2.cloned.1.call-done = bf16[768,192]{0,1:T(8,128)(2,1)} async-done(((bf16[768,6144]{0,1:T(8,128)(2,1)}), bf16[768,192]{0,1:T(8,128)(2,1)}) %reduce-scatter.2.cloned.1.call-update) | async-done | bytes 294928 | tf_op jit(solution)/shard_map/reduce_scatter | solution.py:44
  487.5 1.4 convert_element_type.26
  488.9 0.8 copy.43
  489.7 9.0 %all-to-all-start.2 = ((bf16[8,96,192]{1,2,0:T(8,128)(2,1)}), bf16[8,96,192]{1,2,0:T(8,128)(2,1)S(1)}, u32[]{:S(2)}, u32[]{:S(2)}) async-start(bf16[8,96,192]{1,2,0:T(8,128)(2,1)} %copy.43), calls=%async_computation.3 | async-start | bytes 786432 | tf_op jit(solution)/shard_map/all_to_all | solution.py:48
  498.8 7.7 %all-to-all-done.2 = bf16[8,96,192]{1,2,0:T(8,128)(2,1)S(1)} async-done(((bf16[8,96,192]{1,2,0:T(8,128)(2,1)}), bf16[8,96,192]{1,2,0:T(8,128)(2,1)S(1)}, u32[]{:S(2)}, u32[]{:S(2)}) %all-to-all-start.2) | async-done | bytes 294944 | tf_op jit(solution)/shard_map/all_to_all | solution.py:48
  506.4 1.1 copy.44
  507.5 0.0 copy-start.2
  507.5 0.0 copy-start.3
  507.5 3.4 gather_fusion.1
  510.9 2.1 gather.15
  513.1 0.0 copy-done.2
  513.1 0.0 copy-done.3
  513.1 2.4 multiply_reduce_fusion
  515.5 0.7 copy.46
  (11 shorter events, 0.1 us)
Async XLA Ops:
  6.5 247.8 %copy-start = (bf16[1,256,6144]{2,1,0:T(8,128)(2,1)S(1)}, bf16[1,256,6144]{2,1,0:T(8,128)(2,1)}, u32[]{:S(2)}) copy-start(bf16[1,256,6144]{2,1,0:T(8,128)(2,1)} %param.11) | copy-start | bytes 9437188
  6.5 481.0 %reduce-scatter.2.cloned.1.call-start = ((), (), s32[]{:S(2)}) async-start(), calls=%async_computation.4 | async-start | bytes 9732096 | tf_op jit(solution)/shard_map/reduce_scatter | solution.py:44
  32.1 217.0 %copy-start.1 = (bf16[1,6144,256]{2,1,0:T(8,128)(2,1)S(1)}, bf16[1,6144,256]{2,1,0:T(8,128)(2,1)}, u32[]{:S(2)}) copy-start(bf16[1,6144,256]{2,1,0:T(8,128)(2,1)} %param.9) | copy-start | bytes 9437188
  249.1 2.6 copy-start.6
  259.5 0.7 copy-start.4
  259.5 1.9 copy-start.5
  489.7 16.7 %all-to-all-start.2 = ((bf16[8,96,192]{1,2,0:T(8,128)(2,1)}), bf16[8,96,192]{1,2,0:T(8,128)(2,1)S(1)}, u32[]{:S(2)}, u32[]{:S(2)}) async-start(bf16[8,96,192]{1,2,0:T(8,128)(2,1)} %copy.43), calls=%async_computation.3 | async-start | bytes 786432 | tf_op jit(solution)/shard_map/all_to_all | solution.py:48
  507.5 5.6 %copy-start.2 = (f32[256,2]{1,0:T(8,128)S(1)}, f32[256,2]{1,0:T(8,128)}, u32[]{:S(2)}) copy-start(f32[256,2]{1,0:T(8,128)} %copy.36) | copy-start | bytes 6148
  507.5 5.6 %copy-start.3 = (pred[256,2]{1,0:T(8,128)(4,1)S(1)}, pred[256,2]{1,0:T(8,128)(4,1)}, u32[]{:S(2)}) copy-start(pred[256,2]{1,0:T(8,128)(4,1)} %copy.40) | copy-start | bytes 1540
Sparse Core Ops, SparseCore 0:
  259.6 227.8 reduce-scatter.1
